TPU v7x, 512 devices: a whole 4x8x8 slice. The times are simulated.
512 devices in a mesh: seq: 16 (over y_lo, z), clus: 32 (over x, y_hi, core).
Axes of the slice: x: 4, y: 8 (y_hi: 4, y_lo: 2; y = y_hi * 2 + y_lo), z: 8, core: 2. Of those that a mesh axis runs over, the one named last changes fastest.
Arguments:
- node_feats: bfloat16 [32, 2048, 1024], P('clus', 'seq'), may hold values from -24 to 24
- qkv_weight: bfloat16 [3072, 1024], P('seq'), may hold values from -1 to 1
- block_pairs: int32 [32, 128, 2], P('clus'), may hold values from 0 to 15, as said below
- grad_out: bfloat16 [32, 2048, 1024], P('clus', 'seq'), may hold values from -6 to 6
Outputs:
- attended: bfloat16 [32, 2048, 1024], P('clus', 'seq')
- node_grad: bfloat16 [32, 2048, 1024], P('clus', 'seq')
- weight_grad: float32 [3072, 1024], P('seq')
Inputs may be any that keep to these rules, and one draw needn't show every extreme that they name: `block_pairs`: each cluster's list holds 128 distinct pairs, among them (b, b) for every block b.
All inputs are finite; a program needn't handle non-finite values.
Results may differ from a plain program's by a relative error of at most 0.023.
Values may be sent and summed in bfloat16 or wider, within the bound.
A program may use at most 64 MiB of HBM per device.

v0:
```python
import math
import jax
import jax.numpy as jnp
from jax import lax
from jax.sharding import PartitionSpec as P

HD = 64
BLOCK = 128


def block_allowed(listed, blocks):
    block_ids = jnp.arange(blocks, dtype=jnp.int32)[None, :]
    row_hot = (listed[:, 0:1] == block_ids).astype(jnp.float32)
    col_hot = (listed[:, 1:2] == block_ids).astype(jnp.float32)
    counts = jnp.dot(row_hot.T, col_hot, precision=lax.Precision.HIGHEST)
    return counts > 0.5


def expand_rows(allowed_blocks, offset, row_span):
    picked = lax.dynamic_slice_in_dim(allowed_blocks, offset // BLOCK, row_span // BLOCK, 0)
    return jnp.repeat(jnp.repeat(picked, BLOCK, axis=0), BLOCK, axis=1)


def softmax_rows(query_rows, keys_all, allowed_rows):
    scores = jnp.einsum(
        "qhe,khe->hqk", query_rows, keys_all, preferred_element_type=jnp.float32
    ) * HD ** (-0.5)
    scores = jnp.where(allowed_rows[None], scores, -jnp.inf)
    row_max = jnp.max(scores, axis=-1, keepdims=True)
    unnorm = jnp.where(allowed_rows[None], jnp.exp(scores - row_max), 0.0)
    return unnorm / jnp.sum(unnorm, axis=-1, keepdims=True)


def local(node_feats, qkv_weight, block_pairs, grad_out):
    features = node_feats[0]
    rows_dev = features.shape[0]
    node_count = rows_dev * lax.axis_size("seq")
    columns = qkv_weight.shape[0]
    heads_dev = columns // (3 * HD)
    row_span = math.gcd(node_count, 512)
    offsets = jnp.arange(node_count // row_span, dtype=jnp.int32) * row_span
    projected = lax.dot_general(
        lax.all_gather(features, "seq", axis=0, tiled=True),
        qkv_weight,
        (((1,), (1,)), ((), ())),
        preferred_element_type=jnp.float32,
    ).astype(jnp.bfloat16)
    grouped = projected.reshape(node_count, heads_dev, 3, HD)
    queries = grouped[:, :, 0]
    keys_all = grouped[:, :, 1]
    values_all = grouped[:, :, 2]
    allowed_blocks = block_allowed(block_pairs[0], node_count // BLOCK)

    def forward_block(offset):
        query_rows = lax.dynamic_slice_in_dim(queries, offset, row_span, 0)
        weights = softmax_rows(query_rows, keys_all, expand_rows(allowed_blocks, offset, row_span))
        return jnp.einsum(
            "hqk,khe->qhe",
            weights.astype(jnp.bfloat16),
            values_all,
            preferred_element_type=jnp.float32,
        ).astype(jnp.bfloat16)

    head_out = lax.map(forward_block, offsets).reshape(node_count, heads_dev * HD)
    attended = lax.all_to_all(head_out, "seq", split_axis=0, concat_axis=1, tiled=True)
    upstream = lax.all_to_all(grad_out[0], "seq", split_axis=1, concat_axis=0, tiled=True).reshape(
        node_count, heads_dev, HD
    )

    def backward_block(state_pair, offset):
        grad_keys, grad_values = state_pair
        query_rows = lax.dynamic_slice_in_dim(queries, offset, row_span, 0)
        grad_rows = lax.dynamic_slice_in_dim(upstream, offset, row_span, 0)
        weights = softmax_rows(query_rows, keys_all, expand_rows(allowed_blocks, offset, row_span))
        weights_low = weights.astype(jnp.bfloat16)
        grad_weights = jnp.einsum(
            "qhe,khe->hqk", grad_rows, values_all, preferred_element_type=jnp.float32
        )
        row_delta = jnp.sum(weights * grad_weights, axis=-1, keepdims=True)
        grad_scores = (weights * (grad_weights - row_delta) * HD ** (-0.5)).astype(jnp.bfloat16)
        grad_query = jnp.einsum(
            "hqk,khe->qhe", grad_scores, keys_all, preferred_element_type=jnp.float32
        ).astype(jnp.bfloat16)
        grad_keys = grad_keys + jnp.einsum(
            "hqk,qhe->khe", grad_scores, query_rows, preferred_element_type=jnp.float32
        )
        grad_values = grad_values + jnp.einsum(
            "hqk,qhe->khe", weights_low, grad_rows, preferred_element_type=jnp.float32
        )
        return ((grad_keys, grad_values), grad_query)

    zeros_acc = jnp.zeros((node_count, heads_dev, HD), jnp.float32)
    sums_pair, grad_query = lax.scan(backward_block, (zeros_acc, zeros_acc), offsets)
    grad_query = grad_query.reshape(node_count, heads_dev, HD)
    grad_proj = jnp.stack(
        [grad_query, sums_pair[0].astype(jnp.bfloat16), sums_pair[1].astype(jnp.bfloat16)], axis=2
    ).reshape(node_count, columns)
    rows_part = grad_proj
    node_grad = lax.psum_scatter(
        jnp.dot(rows_part, qkv_weight, preferred_element_type=jnp.float32).astype(jnp.bfloat16),
        "seq",
        scatter_dimension=0,
        tiled=True,
    )
    rows_part = grad_proj
    local_sum = lax.dot_general(
        rows_part,
        lax.all_gather(features, "seq", axis=0, tiled=True),
        (((0,), (0,)), ((), ())),
        preferred_element_type=jnp.float32,
    )
    weight_grad = lax.psum(local_sum.astype(jnp.bfloat16), "clus").astype(
        jnp.float32
    ) / lax.axis_size("clus")
    return (attended[None], node_grad[None], weight_grad)


def solution(mesh):
    return jax.shard_map(
        local,
        mesh=mesh,
        in_specs=(
            P("clus", "seq", None),
            P("seq", None),
            P("clus", None, None),
            P("clus", "seq", None),
        ),
        out_specs=(P("clus", "seq", None), P("clus", "seq", None), P("seq", None)),
        check_vma=False,
    )
```

profile of v0, /device:TPU:6, one launch (start us, length us, event | category | flops | bytes accessed | tf_op | source)
XLA Modules:
  0.0 562.7 jit_solution(15509004296155294109)
XLA Ops:
  7.9 1.8 copy.19
  9.7 11.4 %all-to-all-start.1 = ((bf16[128,16,64]{0,2,1:T(8,128)(2,1)}), bf16[128,16,64]{0,2,1:T(8,128)(2,1)S(1)}, u32[]{:S(2)}, u32[]{:S(2)}) async-start(bf16[128,16,64]{0,2,1:T(8,128)(2,1)} %bitcast.19), calls=%async_computation.1 | async-start | bytes 524288 | tf_op jit(solution)/shard_map/all_to_all | solution.py:66
  22.2 9.6 %all-to-all-done.1 = bf16[128,16,64]{0,2,1:T(8,128)(2,1)S(1)} async-done(((bf16[128,16,64]{0,2,1:T(8,128)(2,1)}), bf16[128,16,64]{0,2,1:T(8,128)(2,1)S(1)}, u32[]{:S(2)}, u32[]{:S(2)}) %all-to-all-start.1) | async-done | bytes 262176 | tf_op jit(solution)/shard_map/all_to_all | solution.py:66
  32.8 61.0 %all-gather.3.cloned.1.call-done = bf16[1,2048,1024]{2,1,0:T(8,128)(2,1)} async-done(((bf16[1,128,1024]{2,1,0:T(8,128)(2,1)}), bf16[1,2048,1024]{2,1,0:T(8,128)(2,1)}) %all-gather.3.cloned.1.call-update) | async-done | bytes 4194320 | tf_op jit(solution)/shard_map/all_gather | solution.py:43
  93.8 3.7 fusion.44
  97.6 0.9 slice_bitcast_fusion
  99.2 88.3 %while.30 = (s32[]{:T(128)}, f32[2048,1,64]{0,2,1:T(8,128)S(1)}, f32[2048,1,64]{0,2,1:T(8,128)S(1)}, bf16[4,512,1,64]{1,3,2,0:T(8,128)(2,1)}, s32[4]{0:T(128)S(1...) while((s32[]{:T(128)}, f32[2048,1,64]{0,2,1:T(8,128)S(1)}, ...), condition=%wide.region_8.9_spmd.clone, body=%wide.region_4.8_spmd.clone.sunk | while | flops 692615680 | bytes 80837776 | solution.py:93
  102.1 3.5 broadcast_in_dim.122
  106.7 2.2 fusion.84
  108.8 1.4 fusion.85
  110.2 3.0 multiply_reduce_fusion.2
  113.3 2.0 copy-done.1
  115.8 1.6 fusion.86
  117.4 2.4 fusion.88
  119.8 1.5 fusion.87
  124.2 3.5 broadcast_in_dim.122
  128.8 2.2 fusion.84
  130.9 1.4 fusion.85
  132.3 3.0 multiply_reduce_fusion.2
  135.4 2.0 copy-done.1
  137.9 1.6 fusion.86
  139.5 2.4 fusion.88
  141.9 1.5 fusion.87
  146.3 3.5 broadcast_in_dim.122
  150.9 2.2 fusion.84
  153.0 1.4 fusion.85
  154.4 3.0 multiply_reduce_fusion.2
  157.5 2.0 copy-done.1
  160.0 1.6 fusion.86
  161.6 2.4 fusion.88
  164.0 1.5 fusion.87
  168.4 3.5 broadcast_in_dim.122
  173.0 2.2 fusion.84
  175.1 1.4 fusion.85
  176.5 3.0 multiply_reduce_fusion.2
  179.6 2.0 copy-done.1
  182.1 1.6 fusion.86
  183.7 2.4 fusion.88
  186.0 1.4 fusion.87
  187.5 1.2 copy.21
  189.0 3.9 fusion.47
  193.2 3.2 convolution_convert_fusion.1
  196.5 56.6 %while.29 = (s32[]{:T(128)}, bf16[4,512,1,64]{1,3,2,0:T(8,128)(2,1)S(1)}, s32[4]{0:T(128)S(1)}, pred[16,16]{1,0:T(8,128)(4,1)S(1)}, bf16[2048,1,64]{0,2,1:T(8,12...) while((s32[]{:T(128)}, ...), condition=%wide.region_3.4_spmd, body=%wide.region_0.3_spmd.sunk | while | flops 283147264 | bytes 17459756 | solution.py:64
  199.8 3.5 broadcast_in_dim.117
  204.5 2.2 fusion.75
  206.7 1.4 fusion.76
  208.1 2.6 fusion.77
  213.9 3.5 broadcast_in_dim.117
  218.7 2.2 fusion.75
  220.8 1.4 fusion.76
  222.2 2.6 fusion.77
  228.1 3.5 broadcast_in_dim.117
  232.8 2.2 fusion.75
  235.0 1.4 fusion.76
  236.4 2.6 fusion.77
  242.2 3.5 broadcast_in_dim.117
  247.0 2.2 fusion.75
  249.1 1.4 fusion.76
  250.5 2.6 fusion.77
  254.2 3.9 all-to-all-start
  258.1 203.0 %all-reduce.2.cloned.1.call-done = bf16[192,1024]{1,0:T(8,128)(2,1)} async-done(((bf16[192,1024]{1,0:T(8,128)(2,1)}), bf16[192,1024]{1,0:T(8,128)(2,1)}) %all-reduce.2.cloned.1.call-update) | async-done | bytes 393232 | tf_op jit(solution)/shard_map/psum | solution.py:112
  461.1 2.0 convert_multiply_fusion
  463.1 0.8 copy.22
  463.9 92.3 %reduce-scatter.2.cloned.1.call-done = bf16[128,1024]{1,0:T(8,128)(2,1)} async-done(((bf16[2048,1024]{1,0:T(8,128)(2,1)}), bf16[128,1024]{1,0:T(8,128)(2,1)}) %reduce-scatter.2.cloned.1.call-update) | async-done | bytes 262160 | tf_op jit(solution)/shard_map/reduce_scatter | solution.py:99
  (64 shorter events, 12.6 us)
Async XLA Ops:
  7.2 86.7 %copy-start = (bf16[192,1024]{1,0:T(8,128)(2,1)S(1)}, bf16[192,1024]{1,0:T(8,128)(2,1)}, u32[]{:S(2)}) copy-start(bf16[192,1024]{1,0:T(8,128)(2,1)} %param.9) | copy-start | bytes 1179652
  7.2 86.7 %all-gather.3.cloned.1.call-start = ((), (), s32[]{:S(2)}) async-start(), calls=%async_computation.5 | async-start | bytes 4456448 | tf_op jit(solution)/shard_map/all_gather | solution.py:43
  9.7 22.1 %all-to-all-start.1 = ((bf16[128,16,64]{0,2,1:T(8,128)(2,1)}), bf16[128,16,64]{0,2,1:T(8,128)(2,1)S(1)}, u32[]{:S(2)}, u32[]{:S(2)}) async-start(bf16[128,16,64]{0,2,1:T(8,128)(2,1)} %bitcast.19), calls=%async_computation.1 | async-start | bytes 524288 | tf_op jit(solution)/shard_map/all_to_all | solution.py:66
  21.1 439.9 %all-reduce.2.cloned.1.call-start = ((), (), s32[]{:S(2)}) async-start(), calls=%async_computation.4 | async-start | bytes 786432 | tf_op jit(solution)/shard_map/psum | solution.py:112
  113.3 2.0 copy-start.1
  115.8 4.0 copy-start.2
  135.4 2.0 copy-start.1
  137.9 4.0 copy-start.2
  157.5 2.0 copy-start.1
  160.0 4.0 copy-start.2
  179.6 2.0 copy-start.1
  182.1 4.0 copy-start.2
  192.9 363.3 %reduce-scatter.2.cloned.1.call-start = ((), (), s32[]{:S(2)}) async-start(), calls=%async_computation.3 | async-start | bytes 4456448 | tf_op jit(solution)/shard_map/reduce_scatter | solution.py:99
  254.2 208.8 %all-to-all-start = ((bf16[16,128,64]{1,2,0:T(8,128)(2,1)}), bf16[16,128,64]{1,2,0:T(8,128)(2,1)S(1)}, u32[]{:S(2)}, u32[]{:S(2)}) async-start(bf16[16,128,64]{1,2,0:T(8,128)(2,1)} %copy.18), calls=%async_computation | async-start | bytes 524288 | tf_op jit(solution)/shard_map/all_to_all | solution.py:65
Sparse Core Ops, SparseCore 0:
  10.1 83.7 all-gather.2
  193.1 267.9 all-reduce.1
  464.5 91.6 reduce-scatter.1
where the time goes:
time: 564 us; the launch traced here: 563 us
  waiting for transfers between devices  367 us (65%)
  matrix products  72.6 us (13%)
  local copies, waits for them, and re-layouts  49.3 us (9%)
  loops' own time  29.3 us (5%)
  starting transfers between devices  15.6 us (3%)
  other arithmetic  15.5 us (3%)
  between operations  13.9 us (2%)
    psum x1, waiting for transfers between devices, local(): lax.psum(local_sum.astype(jnp.bfloat16), 'clus').astype(jnp.float32)  203 us
    reduce_scatter x1, waiting for transfers between devices, local(): lax.psum_scatter(jnp.dot(rows_part, qkv_weight, preferred_element_type=jn...  92.3 us
    all_gather x1, waiting for transfers between devices, local(): lax.all_gather(features, 'seq', axis=0, tiled=True)  61 us
    broadcast_in_dim x16, local copies, waits for them, and re-layouts, expand_rows(): return jnp.repeat(jnp.repeat(picked, BLOCK, axis=0), BLOCK, axis=1)  27.9 us
    dot_general x8, matrix products, softmax_rows(): jnp.einsum('qhe,khe->hqk', query_rows, keys_all, preferred_element_type=j...  17.3 us
    another operation x1, loops' own time, local(): lax.map(forward_block, offsets).reshape(node_count, heads_dev * HD)  15.5 us
    another operation x1, loops' own time, local(): lax.scan(backward_block, (zeros_acc, zeros_acc), offsets)  13.8 us
    dot_general x4, matrix products, backward_block(): jnp.einsum('qhe,khe->hqk', grad_rows, values_all, preferred_element_type=...  12.1 us
  transfers between devices with their start and end apart: 5, of which 4 were waited for; matrix products, arithmetic and copies ran while one was open for 9% of the time, Pallas kernels for 0%

commit v1 on v0

--- a/solution.py
+++ b/solution.py
@@ -1,3 +1,4 @@
+import functools
 import math
 import jax
 import jax.numpy as jnp
@@ -6,6 +7,14 @@
 
 HD = 64
 BLOCK = 128
+
+
+def read_regions_by_axis(original, mesh_ax):
+    outer = lax.all_gather(original, mesh_ax).sum(axis=0)
+    return outer
+
+
+waves_group = functools.partial(read_regions_by_axis, mesh_ax="clus")
 
 
 def block_allowed(listed, blocks):
@@ -109,9 +118,9 @@
         (((0,), (0,)), ((), ())),
         preferred_element_type=jnp.float32,
     )
-    weight_grad = lax.psum(local_sum.astype(jnp.bfloat16), "clus").astype(
-        jnp.float32
-    ) / lax.axis_size("clus")
+    weight_grad = waves_group(local_sum.astype(jnp.bfloat16)).astype(jnp.float32) / lax.axis_size(
+        "clus"
+    )
     return (attended[None], node_grad[None], weight_grad)
 
 

time: 564 us -> 396 us (0.70)
  waiting for transfers between devices: 367 us -> 171 us
  blocking collectives: 0 us -> 19.7 us
  other arithmetic: 15.5 us -> 22.3 us
    psum x1 -> x0, waiting for transfers between devices: 203 us -> none  [local(): lax.psum(local_sum.astype(jnp.bfloat16), 'clus').astype(jnp.float32)]
    all_gather x0 -> x1, waiting for transfers between devices: none -> 21.1 us  [read_regions_by_axis(): outer = lax.all_gather(original, mesh_ax).sum(axis=0)]
    all_to_all x0 -> x1, blocking collectives: none -> 19.7 us  [local(): lax.all_to_all(head_out, 'seq', split_axis=0, concat_axis=1, tiled=True)]
    reduce_scatter x1, waiting for transfers between devices: 92.3 us -> 78.9 us  [local(): lax.psum_scatter(jnp.dot(rows_part, qkv_weight, preferred_element_type=jn...]
    reduce_sum x0 -> x1, other arithmetic: none -> 7.87 us  [read_regions_by_axis(): outer = lax.all_gather(original, mesh_ax).sum(axis=0)]
  transfers between devices with their start and end apart: 5 -> 4, of which waited for: 4 -> 4; matrix products, arithmetic and copies ran while one was open for 9% -> 15% of each run, Pallas kernels for 0% -> 0%
where the time goes in v1:
time: 396 us; the launch traced here: 394 us
  waiting for transfers between devices  171 us (43%)
  matrix products  72.7 us (18%)
  local copies, waits for them, and re-layouts  49 us (12%)
  loops' own time  33.8 us (9%)
  other arithmetic  22.3 us (6%)
  blocking collectives  19.7 us (5%)
  between operations  13.9 us (4%)
  starting transfers between devices  11.7 us (3%)
    reduce_scatter x1, waiting for transfers between devices, local(): lax.psum_scatter(jnp.dot(rows_part, qkv_weight, preferred_element_type=jn...  78.9 us
    all_gather x1, waiting for transfers between devices, local(): lax.all_gather(features, 'seq', axis=0, tiled=True)  61 us
    broadcast_in_dim x16, local copies, waits for them, and re-layouts, expand_rows(): return jnp.repeat(jnp.repeat(picked, BLOCK, axis=0), BLOCK, axis=1)  27.9 us
    all_gather x1, waiting for transfers between devices, read_regions_by_axis(): outer = lax.all_gather(original, mesh_ax).sum(axis=0)  21.1 us
    all_to_all x1, blocking collectives, local(): lax.all_to_all(head_out, 'seq', split_axis=0, concat_axis=1, tiled=True)  19.7 us
    dot_general x8, matrix products, softmax_rows(): jnp.einsum('qhe,khe->hqk', query_rows, keys_all, preferred_element_type=j...  17.3 us
    another operation x1, loops' own time, local(): lax.scan(backward_block, (zeros_acc, zeros_acc), offsets)  17 us
    another operation x1, loops' own time, local(): lax.map(forward_block, offsets).reshape(node_count, heads_dev * HD)  16.8 us
  transfers between devices with their start and end apart: 4, of which 4 were waited for; matrix products, arithmetic and copies ran while one was open for 15% of the time, Pallas kernels for 0%

profile of v1, /device:TPU:6, one launch (start us, length us, event | category | flops | bytes accessed | tf_op | source)
XLA Modules:
  0.0 394.4 jit_solution(14721656960751760977)
XLA Ops:
  7.9 1.8 copy.19
  9.7 11.4 %all-to-all-start.1 = ((bf16[128,16,64]{0,2,1:T(8,128)(2,1)}), bf16[128,16,64]{0,2,1:T(8,128)(2,1)S(1)}, u32[]{:S(2)}, u32[]{:S(2)}) async-start(bf16[128,16,64]{0,2,1:T(8,128)(2,1)} %bitcast.19), calls=%async_computation.1 | async-start | bytes 524288 | tf_op jit(solution)/shard_map/all_to_all | solution.py:75
  22.2 9.6 %all-to-all-done.1 = bf16[128,16,64]{0,2,1:T(8,128)(2,1)S(1)} async-done(((bf16[128,16,64]{0,2,1:T(8,128)(2,1)}), bf16[128,16,64]{0,2,1:T(8,128)(2,1)S(1)}, u32[]{:S(2)}, u32[]{:S(2)}) %all-to-all-start.1) | async-done | bytes 262176 | tf_op jit(solution)/shard_map/all_to_all | solution.py:75
  32.8 61.0 %all-gather.5.cloned.1.call-done = bf16[1,2048,1024]{2,1,0:T(8,128)(2,1)} async-done(((bf16[1,128,1024]{2,1,0:T(8,128)(2,1)}), bf16[1,2048,1024]{2,1,0:T(8,128)(2,1)}) %all-gather.5.cloned.1.call-update) | async-done | bytes 4194320 | tf_op jit(solution)/shard_map/all_gather | solution.py:52
  93.8 3.7 fusion.44
  97.6 0.9 slice_bitcast_fusion
  99.2 91.8 %while.30 = (s32[]{:T(128)}, f32[2048,1,64]{0,2,1:T(8,128)S(1)}, f32[2048,1,64]{0,2,1:T(8,128)S(1)}, bf16[4,512,1,64]{1,3,2,0:T(8,128)(2,1)}, s32[4]{0:T(128)S(1...) while((s32[]{:T(128)}, f32[2048,1,64]{0,2,1:T(8,128)S(1)}, ...), condition=%wide.region_8.9_spmd.clone, body=%wide.region_4.8_spmd.clone.sunk | while | flops 692615680 | bytes 80837776 | solution.py:102
  102.7 3.5 broadcast_in_dim.122
  107.5 2.2 fusion.84
  109.7 1.4 fusion.85
  111.1 3.0 multiply_reduce_fusion.2
  114.1 2.0 copy-done.1
  116.6 1.6 fusion.86
  118.3 2.4 fusion.88
  120.6 1.5 fusion.87
  125.6 3.5 broadcast_in_dim.122
  130.5 2.2 fusion.84
  132.6 1.4 fusion.85
  134.0 3.0 multiply_reduce_fusion.2
  137.1 2.0 copy-done.1
  139.6 1.6 fusion.86
  141.3 2.4 fusion.88
  143.6 1.5 fusion.87
  148.6 3.5 broadcast_in_dim.122
  153.5 2.2 fusion.84
  155.6 1.4 fusion.85
  157.0 3.0 multiply_reduce_fusion.2
  160.1 2.0 copy-done.1
  162.6 1.6 fusion.86
  164.2 2.4 fusion.88
  166.6 1.5 fusion.87
  171.6 3.5 broadcast_in_dim.122
  176.4 2.2 fusion.84
  178.6 1.4 fusion.85
  180.0 3.0 multiply_reduce_fusion.2
  183.0 2.0 copy-done.1
  185.5 1.6 fusion.86
  187.1 2.4 fusion.88
  189.5 1.4 fusion.87
  190.9 1.2 copy.21
  192.4 3.9 fusion.47
  196.6 3.3 convolution_convert_fusion.1
  199.9 58.1 %while.29 = (s32[]{:T(128)}, bf16[4,512,1,64]{1,3,2,0:T(8,128)(2,1)S(1)}, s32[4]{0:T(128)S(1)}, pred[16,16]{1,0:T(8,128)(4,1)S(1)}, bf16[2048,1,64]{0,2,1:T(8,12...) while((s32[]{:T(128)}, ...), condition=%wide.region_3.4_spmd, body=%wide.region_0.3_spmd.sunk | while | flops 283147264 | bytes 17459756 | solution.py:73
  203.4 3.5 broadcast_in_dim.117
  208.3 2.2 fusion.75
  210.5 1.4 fusion.76
  211.9 2.6 fusion.77
  218.0 3.5 broadcast_in_dim.117
  222.8 2.2 fusion.75
  225.0 1.4 fusion.76
  226.4 2.6 fusion.77
  232.5 3.5 broadcast_in_dim.117
  237.3 2.2 fusion.75
  239.5 1.4 fusion.76
  240.9 2.6 fusion.77
  247.1 3.5 broadcast_in_dim.117
  251.9 2.2 fusion.75
  254.1 1.4 fusion.76
  255.5 2.6 fusion.77
  258.5 19.7 %all_to_all.32 = bf16[16,128,64]{1,2,0:T(8,128)(2,1)S(1)} all-to-all(bf16[16,128,64]{1,2,0:T(8,128)(2,1)S(1)} %copy.18), channel_id=1, replica_groups=mesh['seq'=16,'clus'=32] {'seq'}, dimensions={0} | all-to-all | bytes 524288 | tf_op jit(solution)/shard_map/all_to_all | solution.py:74
  279.0 21.1 %all-gather.7.cloned.1.call-done = bf16[6144,1024]{1,0:T(8,128)(2,1)} async-done(((bf16[192,1024]{1,0:T(8,128)(2,1)}), bf16[6144,1024]{1,0:T(8,128)(2,1)}) %all-gather.7.cloned.1.call-update) | async-done | bytes 12582928 | tf_op jit(solution)/shard_map/all_gather | solution.py:13
  300.1 7.9 %reduce_sum.39 = bf16[192,1024]{1,0:T(8,128)(2,1)S(1)} reduce(bf16[32,192,1024]{2,1,0:T(8,128)(2,1)} %bitcast.212, bf16[]{:T(256)} %constant.141.clone.1), dimensions={0}, to_apply=%region_10.11 | reduce | flops 6094848 | bytes 12976130 | tf_op jit(solution)/shard_map/reduce_sum | solution.py:13
  308.0 1.0 convert_multiply_fusion
  308.9 78.9 %reduce-scatter.2.cloned.1.call-done = bf16[128,1024]{1,0:T(8,128)(2,1)} async-done(((bf16[2048,1024]{1,0:T(8,128)(2,1)}), bf16[128,1024]{1,0:T(8,128)(2,1)}) %reduce-scatter.2.cloned.1.call-update) | async-done | bytes 262160 | tf_op jit(solution)/shard_map/reduce_scatter | solution.py:108
  (64 shorter events, 13.2 us)
Async XLA Ops:
  7.2 86.7 %copy-start = (bf16[192,1024]{1,0:T(8,128)(2,1)S(1)}, bf16[192,1024]{1,0:T(8,128)(2,1)}, u32[]{:S(2)}) copy-start(bf16[192,1024]{1,0:T(8,128)(2,1)} %param.9) | copy-start | bytes 1179652
  7.2 86.7 %all-gather.5.cloned.1.call-start = ((), (), s32[]{:S(2)}) async-start(), calls=%async_computation.4 | async-start | bytes 4456448 | tf_op jit(solution)/shard_map/all_gather | solution.py:52
  9.7 22.1 %all-to-all-start.1 = ((bf16[128,16,64]{0,2,1:T(8,128)(2,1)}), bf16[128,16,64]{0,2,1:T(8,128)(2,1)S(1)}, u32[]{:S(2)}, u32[]{:S(2)}) async-start(bf16[128,16,64]{0,2,1:T(8,128)(2,1)} %bitcast.19), calls=%async_computation.1 | async-start | bytes 524288 | tf_op jit(solution)/shard_map/all_to_all | solution.py:75
  21.1 278.9 %all-gather.7.cloned.1.call-start = ((), (), s32[]{:S(2)}) async-start(), calls=%async_computation.5 | async-start | bytes 12976128 | tf_op jit(solution)/shard_map/all_gather | solution.py:13
  114.1 2.0 copy-start.1
  116.6 4.0 %copy-start.2 = (f32[512,2048]{1,0:T(8,128)S(1)}, f32[512,2048]{1,0:T(8,128)}, u32[]{:S(2)}) copy-start(f32[512,2048]{1,0:T(8,128)} %copy-done.1) | copy-start | bytes 12582916 | tf_op jit(solution)/shard_map/while
  137.1 2.0 copy-start.1
  139.6 4.0 %copy-start.2 = (f32[512,2048]{1,0:T(8,128)S(1)}, f32[512,2048]{1,0:T(8,128)}, u32[]{:S(2)}) copy-start(f32[512,2048]{1,0:T(8,128)} %copy-done.1) | copy-start | bytes 12582916 | tf_op jit(solution)/shard_map/while
  160.1 2.0 copy-start.1
  162.6 4.0 %copy-start.2 = (f32[512,2048]{1,0:T(8,128)S(1)}, f32[512,2048]{1,0:T(8,128)}, u32[]{:S(2)}) copy-start(f32[512,2048]{1,0:T(8,128)} %copy-done.1) | copy-start | bytes 12582916 | tf_op jit(solution)/shard_map/while
  183.0 2.0 copy-start.1
  185.5 4.0 %copy-start.2 = (f32[512,2048]{1,0:T(8,128)S(1)}, f32[512,2048]{1,0:T(8,128)}, u32[]{:S(2)}) copy-start(f32[512,2048]{1,0:T(8,128)} %copy-done.1) | copy-start | bytes 12582916 | tf_op jit(solution)/shard_map/while
  196.4 191.5 %reduce-scatter.2.cloned.1.call-start = ((), (), s32[]{:S(2)}) async-start(), calls=%async_computation.3 | async-start | bytes 4456448 | tf_op jit(solution)/shard_map/reduce_scatter | solution.py:108
Sparse Core Ops, SparseCore 0:
  10.1 83.7 all-gather.4
  196.5 103.5 all-gather.6
  303.5 84.3 reduce-scatter.1
